TPU v7x, 32 devices: a whole 2x2x4 slice. The times are simulated.
32 devices in a mesh: ctx: 8 (over z, x), head: 4 (over y, core).
Axes of the slice: x: 2, y: 2, z: 4, core: 2. Of those that a mesh axis runs over, the one named last changes fastest.
Arguments:
- attn_query: bfloat16 [4096, 6144], P('ctx', 'head'), may hold values from -16 to 16
- attn_key: bfloat16 [4096, 6144], P('ctx', 'head'), may hold values from -16 to 16
- attn_value: bfloat16 [4096, 6144], P('ctx', 'head'), may hold values from -120 to 120
- delta_query: bfloat16 [4096, 6144], P('ctx', 'head'), may hold values from -6 to 6
- delta_key: bfloat16 [4096, 6144], P('ctx', 'head'), may hold values from -6 to 6
- delta_value: bfloat16 [4096, 6144], P('ctx', 'head'), may hold values from -120 to 120
- delta_gate: float32 [4096, 48], P('ctx', 'head'), may hold values from 0.5 to 1
- delta_beta: float32 [4096, 48], P('ctx', 'head'), may hold values from 0 to 0.6, as said below
- attn_gain: float32 [6144], P('head'), may hold values from 0.1 to 1.9
- delta_gain: float32 [6144], P('head'), may hold values from 0.1 to 1.9
Outputs:
- mixed: bfloat16 [4096, 6144], P('ctx', 'head')
Inputs may be any that keep to these rules, and one draw needn't show every extreme that they name: `delta_beta`: Positive.
All inputs are finite; a program needn't handle non-finite values.
Results may differ from a plain program's by a relative error of at most 0.004.
Values may be sent and summed in bfloat16 or wider, within the bound.
A program may use at most 192 MiB of HBM per device.

v0:
```python
import functools
import math

import jax
import jax.numpy as jnp
from jax import lax
from jax.experimental import pallas as pl
from jax.experimental.pallas import tpu as pltpu
from jax.sharding import PartitionSpec as P

DH = 128
WINDOW = 1024
CHUNK = 128
QROWS = 256
HALO_AHEAD = 1
RELAY_LAG = 5
HEADS_STEP = 2

epsilon = 1e-06
f32 = jnp.float32
bf16 = jnp.bfloat16


def dot(left, right, dims=((1,), (0,))):
    return lax.dot_general(left, right, (dims, ((), ())), preferred_element_type=f32)


def dot1(left, right, dims=((1,), (0,))):
    return dot(left.astype(bf16), right.astype(bf16), dims)


def split(value):
    high = value.astype(bf16)
    return high, (value - high.astype(f32)).astype(bf16)


def dot3(left, right, dims=((1,), (0,))):
    lh, ll = split(left)
    rh, rl = split(right)
    return dot(lh, rh, dims) + (dot(lh, rl, dims) + dot(ll, rh, dims))


def unit_scale(raw):
    wide = raw.astype(f32)
    mean = jnp.mean(wide * wide, axis=-1, keepdims=True)
    return lax.rsqrt(mean + epsilon) / math.sqrt(DH)


def delta_heads(first, q_ref, k_ref, v_ref, gate_ref, beta_ref, out_ref, qeff_ref, lin_ref, off_ref):
    rows = q_ref.shape[0]
    chunks = rows // CHUNK
    ri = lax.broadcasted_iota(jnp.int32, (CHUNK, CHUNK), 0)
    ci = lax.broadcasted_iota(jnp.int32, (CHUNK, CHUNK), 1)
    eye = ri == ci
    lower = ri >= ci
    strict = ri > ci
    identity = jnp.where(eye, 1.0, 0.0).astype(f32)

    def column(row):
        return jnp.sum(jnp.where(eye, row, 0.0), axis=1, keepdims=True)

    def as_row(col):
        return jnp.sum(jnp.where(eye, col, 0.0), axis=0, keepdims=True)

    units = [(h, c) for c in range(chunks) for h in range(HEADS_STEP)]
    terms = {}
    for h, c in units:
        rs = slice(c * CHUNK, (c + 1) * CHUNK)
        cs = pl.ds(pl.multiple_of((first + h) * DH, DH), DH)
        q, k = q_ref[rs, cs], k_ref[rs, cs]
        log_row = jnp.log(gate_ref[first + h, :, rs])
        log_col = column(log_row)
        beta_col = column(beta_ref[first + h, :, rs])
        sum_row = jnp.sum(jnp.where(ri <= ci, log_col, 0.0), axis=0, keepdims=True)
        sum_col = jnp.sum(jnp.where(lower, log_row, 0.0), axis=1, keepdims=True)
        total = jnp.sum(log_row, axis=1, keepdims=True)
        sk, sq = unit_scale(k), unit_scale(q)
        sk_row = as_row(sk)
        ratios = jnp.exp(jnp.where(lower, sum_col - sum_row, -1e30)) * sk_row
        both = dot(jnp.concatenate([k, q], axis=0), k, ((1,), (1,)))
        low = jnp.where(strict, (beta_col * sk) * ratios * both[:CHUNK], 0.0)
        mix = (sq * ratios) * both[CHUNK:]
        growth = jnp.exp(sum_col)
        terms[h, c] = dict(
            low=low,
            mix=mix.astype(bf16),
            inv=identity - jnp.where((ri // 2) == (ci // 2), low, 0.0),
            beta=beta_col,
            gk=growth * sk,
            gq=growth * sq,
            tail=jnp.exp(total - sum_col) * sk,
            last=jnp.exp(total),
        )
    size = 2
    while size < CHUNK:
        pick = ((ri // (2 * size)) == (ci // (2 * size))) & ((ri // size) != (ci // size))
        for u in units:
            t = terms[u]
            t["tmp"] = dot1(jnp.where(pick, t["low"], 0.0), t["inv"])
        for u in units:
            t = terms[u]
            t["inv"] = t["inv"] - dot1(t["inv"], t["tmp"])
        size *= 2
    states = [None] * HEADS_STEP
    for c in range(chunks):
        rs = slice(c * CHUNK, (c + 1) * CHUNK)
        for h in range(HEADS_STEP):
            cs = pl.ds(pl.multiple_of((first + h) * DH, DH), DH)
            t = terms[h, c]
            q, k, v = q_ref[rs, cs], k_ref[rs, cs], v_ref[rs, cs].astype(f32)
            zero = jnp.zeros((CHUNK, DH), f32)
            if c == 0:
                state = jnp.concatenate([jnp.zeros((DH, DH), f32), identity], axis=1)
                ks = jnp.concatenate([zero, k.astype(f32)], axis=1)
                qs = jnp.concatenate([zero, q.astype(f32)], axis=1)
            else:
                state = states[h]
                sb = state.astype(bf16)
                kqs = dot(jnp.concatenate([k, q], axis=0), sb)
                ks, qs = kqs[:CHUNK], kqs[CHUNK:]
            resid = jnp.concatenate([v, zero], axis=1) - t["gk"] * ks
            errors = dot1(t["inv"], t["beta"] * resid)
            out = t["gq"] * qs + dot(t["mix"], errors.astype(bf16))
            out_ref[first + h, rs] = out[:, :DH]
            qeff_ref[first + h, rs] = out[:, DH:].astype(bf16)
            states[h] = t["last"] * state + dot(
                k, (t["tail"] * errors).astype(bf16), ((0,), (0,))
            )
    for h in range(HEADS_STEP):
        off_ref[first + h] = states[h][:, :DH]
        lin_ref[first + h] = states[h][:, DH:]


def layer_kernel(
    aq_ref, ak_ref, av_ref, dq_ref, dk_ref, dv_ref, gates_ref, betas_ref, again_ref, dgain_ref,
    mixed_hbm,
    keys, vals, attn_out, delta_out, qeff, linear, offset, entering, leaving, attn_sq, delta_sq,
    sums_send, sums_recv, gate_ref, beta_ref, mixed_ref,
    out_sem, own_sem, far_send, far_recv, near_send, near_recv, relay_send, relay_recv, sums_ss, sums_rs,
    *, contexts, groups,
):
    rows, width = aq_ref.shape
    heads = width // DH
    me = lax.axis_index("ctx")
    group = lax.axis_index("head")
    odd = lax.rem(me, 2) == 1
    even = lax.rem(me, 2) == 0
    back = WINDOW
    halves = rows // QROWS
    blocks = rows // CHUNK

    both = ((0, ak_ref, keys), (1, av_ref, vals))
    far_rows = pl.ds(0, rows)
    near_rows = pl.ds(rows, rows)
    own_rows = pl.ds(back, rows)

    def lanes(h):
        return pl.ds(pl.multiple_of(h * DH, DH), DH)

    def own_copy(h, kind, source, buffer):
        return pltpu.make_async_copy(
            source.at[:, lanes(h)], buffer.at[h, own_rows], own_sem.at[kind, h]
        )

    def far_copy(h, kind, source, buffer):
        return pltpu.make_async_remote_copy(
            src_ref=buffer.at[h, own_rows],
            dst_ref=buffer.at[h, far_rows],
            send_sem=far_send.at[kind, h],
            recv_sem=far_recv.at[kind, h],
            device_id={"ctx": lax.rem(me + 2, contexts)},
            device_id_type=pl.DeviceIdType.MESH,
        )

    def near_copy(h, kind, source, buffer):
        return pltpu.make_async_remote_copy(
            src_ref=buffer.at[h, own_rows],
            dst_ref=buffer.at[h, near_rows],
            send_sem=near_send.at[kind, h],
            recv_sem=near_recv.at[kind, h],
            device_id={"ctx": lax.rem(me + 1, contexts)},
            device_id_type=pl.DeviceIdType.MESH,
        )

    def forward_copy(h, kind, source, buffer):
        return pltpu.make_async_remote_copy(
            src_ref=buffer.at[h, far_rows],
            dst_ref=buffer.at[h, near_rows],
            send_sem=near_send.at[kind, h],
            recv_sem=near_recv.at[kind, h],
            device_id={"ctx": lax.rem(me + contexts - 1, contexts)},
            device_id_type=pl.DeviceIdType.MESH,
        )

    def relay_copy(h):
        return pltpu.make_async_remote_copy(
            src_ref=leaving.at[h],
            dst_ref=entering.at[h],
            send_sem=relay_send.at[h],
            recv_sem=relay_recv.at[h],
            device_id={"ctx": lax.rem(me + 1, contexts)},
            device_id_type=pl.DeviceIdType.MESH,
        )

    def send_halo(h):
        @pl.when(h < heads)
        def _():
            @pl.when(me + 2 < contexts)
            def _():
                for args in both:
                    far_copy(h, *args).start()

            @pl.when(even)
            def _():
                for args in both:
                    near_copy(h, *args).start()

    def forward(h):
        @pl.when(odd & (me >= 3))
        def _():
            for args in both:
                far_copy(h, *args).wait_recv()
                forward_copy(h, *args).start()

    def start_own(h, carry):
        for args in both:
            own_copy(h, *args).start()
        return carry

    lax.fori_loop(0, heads, start_own, 0)

    barrier = pltpu.get_barrier_semaphore()
    for by in (-2, -1, 1, 2):
        @pl.when((me + by >= 0) & (me + by < contexts))
        def _():
            pl.semaphore_signal(
                barrier, inc=1, device_id={"ctx": me + by}, device_id_type=pl.DeviceIdType.MESH
            )
    for by in range(1, groups):
        pl.semaphore_signal(
            barrier, inc=1, device_id={"head": lax.rem(group + by, groups)},
            device_id_type=pl.DeviceIdType.MESH,
        )
    near_peers = jnp.minimum(me, 2) + jnp.minimum(contexts - 1 - me, 2)
    pl.semaphore_wait(barrier, near_peers + (groups - 1))

    def wait_own(h, carry):
        for args in both:
            own_copy(h, *args).wait()
        return carry

    lax.fori_loop(0, heads, wait_own, 0)
    lax.fori_loop(0, min(HALO_AHEAD, heads), lambda h, c: (send_halo(h), c)[1], 0)

    @pl.when(me < 2)
    def _():
        def clear(h, carry):
            keys[h, far_rows] = jnp.zeros((rows, DH), bf16)
            vals[h, far_rows] = jnp.zeros((rows, DH), bf16)
            return carry
        lax.fori_loop(0, heads, clear, 0)

    @pl.when(me < 1)
    def _():
        def clear(h, carry):
            keys[h, near_rows] = jnp.zeros((rows, DH), bf16)
            vals[h, near_rows] = jnp.zeros((rows, DH), bf16)
            entering[h] = jnp.zeros((DH, DH), f32)
            return carry
        lax.fori_loop(0, heads, clear, 0)

    gate_rows, beta_rows = gates_ref[...].T, betas_ref[...].T
    for h in range(heads):
        gate_ref[h] = gate_rows[h : h + 1]
        beta_ref[h] = beta_rows[h : h + 1]
    attn_sq[...] = jnp.zeros_like(attn_sq)
    delta_sq[...] = jnp.zeros_like(delta_sq)
    steps = heads // HEADS_STEP

    def delta_step(i, carry):
        delta_heads(
            i * HEADS_STEP, dq_ref, dk_ref, dv_ref, gate_ref, beta_ref,
            delta_out, qeff, linear, offset,
        )

        @pl.when(i >= 1)
        def _():
            forward(i - 1)

        send_halo(HALO_AHEAD + i)
        return carry

    lax.fori_loop(0, steps, delta_step, 0)

    scale = math.log2(math.e) / math.sqrt(DH)
    ri = lax.broadcasted_iota(jnp.int32, (QROWS, QROWS), 0)
    ci = lax.broadcasted_iota(jnp.int32, (QROWS, QROWS), 1)
    tiles = WINDOW // QROWS + 1
    first_tile = jnp.maximum(WINDOW - me * rows, 0) // QROWS

    def attend(h, b):
        q_rows = pl.ds(pl.multiple_of(b * QROWS, QROWS), QROWS)
        q = aq_ref[q_rows, lanes(h)]
        scores = []
        for n in range(tiles):
            at = pl.ds(pl.multiple_of((b + n) * QROWS, QROWS), QROWS)
            s = dot(q, keys[h, at], ((1,), (1,))) * scale
            if n < tiles - 1:
                s = s + jnp.where(b + n >= first_tile, 0.0, -1e30).astype(f32)
            if n == 0:
                s = jnp.where(ci > ri, s, -1e30)
            if n == tiles - 1:
                s = jnp.where(ci <= ri, s, -1e30)
            scores.append(s)
        top = jnp.max(functools.reduce(jnp.maximum, scores), axis=1, keepdims=True)
        raised = [jnp.exp2(s - top) for s in scores]
        total = jnp.sum(functools.reduce(jnp.add, raised), axis=1, keepdims=True)
        inverse = 1.0 / total
        out = None
        for n in range(tiles):
            at = pl.ds(pl.multiple_of((b + n) * QROWS, QROWS), QROWS)
            part = dot((raised[n] * inverse).astype(bf16), vals[h, at])
            out = part if out is None else out + part
        attn_out[h, q_rows] = out
        attn_sq[q_rows, :] += out * out

    def relay(h):
        @pl.when(me >= 1)
        def _():
            relay_copy(h).wait_recv()

        state = entering[h]

        @pl.when(me + 1 < contexts)
        def _():
            leaving[h] = dot3(linear[h], state) + offset[h]
            relay_copy(h).start()

        high, low = split(state)
        q = qeff[h]
        full = delta_out[h] + (dot(q, high) + dot(q, low))
        delta_out[h] = full
        delta_sq[...] += full * full

    def step(j, carry):
        h, b = j // halves, lax.rem(j, halves)

        @pl.when(h < heads)
        def _():
            @pl.when(b == 0)
            def _():
                @pl.when(h >= steps - 1)
                def _():
                    forward(h)

                for args in both:
                    @pl.when((me >= 2) & jnp.logical_not(odd & (me >= 3)))
                    def _():
                        far_copy(h, *args).wait_recv()

                    @pl.when(me >= 1)
                    def _():
                        near_copy(h, *args).wait_recv()

                send_halo(h + HALO_AHEAD + steps)

            attend(h, b)

        r = j - RELAY_LAG * me

        @pl.when((r >= 0) & (r < heads))
        def _():
            relay(r)

        return carry

    turns = max(heads * halves, RELAY_LAG * (contexts - 1) + heads)
    lax.fori_loop(0, turns, step, 0)

    dr = lax.broadcasted_iota(jnp.int32, (CHUNK, CHUNK), 0)
    dc = lax.broadcasted_iota(jnp.int32, (CHUNK, CHUNK), 1)
    eye = dr == dc
    lines = []
    for part in (attn_sq, delta_sq):
        for b in range(blocks):
            col = jnp.sum(part[b * CHUNK : (b + 1) * CHUNK, :], axis=1, keepdims=True)
            lines.append(jnp.sum(jnp.where(eye, col, 0.0), axis=0, keepdims=True))
    mine = jnp.concatenate(lines, axis=0)
    sums_send[...] = mine

    def sums_copy(by):
        return pltpu.make_async_remote_copy(
            src_ref=sums_send,
            dst_ref=sums_recv.at[by],
            send_sem=sums_ss.at[by],
            recv_sem=sums_rs.at[by],
            device_id={"head": lax.rem(group + by, groups)},
            device_id_type=pl.DeviceIdType.MESH,
        )

    for by in range(1, groups):
        sums_copy(by).start()
    whole = mine
    for by in range(1, groups):
        sums_copy(by).wait_recv()
        whole = whole + sums_recv[by]
    scales = lax.rsqrt(whole / (width * groups) + epsilon) * 0.5

    def out_copy(b):
        span = pl.ds(b * CHUNK, CHUNK)
        return pltpu.make_async_copy(mixed_ref.at[span], mixed_hbm.at[span], out_sem.at[b])

    for b in range(blocks):
        rs = slice(b * CHUNK, (b + 1) * CHUNK)
        sa = jnp.sum(jnp.where(eye, scales[b : b + 1], 0.0), axis=1, keepdims=True)
        sd = jnp.sum(
            jnp.where(eye, scales[blocks + b : blocks + b + 1], 0.0), axis=1, keepdims=True
        )
        for h in range(heads):
            cs = slice(h * DH, (h + 1) * DH)
            mixed_ref[rs, cs] = (
                again_ref[cs][None, :] * attn_out[h, rs] * sa + dgain_ref[cs][None, :] * delta_out[h, rs] * sd
            ).astype(bf16)
        out_copy(b).start()

    for b in range(blocks):
        out_copy(b).wait()
    for by in range(1, groups):
        sums_copy(by).wait_send()

    def drain(h, carry):
        for args in both:
            @pl.when(me + 2 < contexts)
            def _():
                far_copy(h, *args).wait_send()

            @pl.when(even)
            def _():
                near_copy(h, *args).wait_send()

            @pl.when(odd & (me >= 3))
            def _():
                forward_copy(h, *args).wait_send()

        @pl.when(me + 1 < contexts)
        def _():
            relay_copy(h).wait_send()

        return carry

    lax.fori_loop(0, heads, drain, 0)


def on_device(
    attn_query,
    attn_key,
    attn_value,
    delta_query,
    delta_key,
    delta_value,
    delta_gate,
    delta_beta,
    attn_gain,
    delta_gain,
):
    rows, width = attn_query.shape
    heads = width // DH
    groups = lax.axis_size("head")
    lines = 2 * rows // CHUNK
    vmem = pl.BlockSpec(memory_space=pltpu.VMEM)
    hbm = pl.BlockSpec(memory_space=pl.ANY)
    dma = pltpu.SemaphoreType.DMA
    return pl.pallas_call(
        functools.partial(layer_kernel, contexts=lax.axis_size("ctx"), groups=groups),
        in_specs=[vmem, hbm, hbm] + [vmem] * 7,
        out_specs=hbm,
        out_shape=jax.ShapeDtypeStruct((rows, width), bf16),
        scratch_shapes=[
            pltpu.VMEM((heads, WINDOW + rows, DH), bf16),
            pltpu.VMEM((heads, WINDOW + rows, DH), bf16),
            pltpu.VMEM((heads, rows, DH), f32),
            pltpu.VMEM((heads, rows, DH), f32),
            pltpu.VMEM((heads, rows, DH), bf16),
            pltpu.VMEM((heads, DH, DH), f32),
            pltpu.VMEM((heads, DH, DH), f32),
            pltpu.VMEM((heads, DH, DH), f32),
            pltpu.VMEM((heads, DH, DH), f32),
            pltpu.VMEM((rows, DH), f32),
            pltpu.VMEM((rows, DH), f32),
            pltpu.VMEM((lines, CHUNK), f32),
            pltpu.VMEM((groups, lines, CHUNK), f32),
            pltpu.VMEM((heads, 1, rows), f32),
            pltpu.VMEM((heads, 1, rows), f32),
            pltpu.VMEM((rows, width), bf16),
            dma((rows // CHUNK,)),
            dma((2, heads)),
            dma((2, heads)),
            dma((2, heads)),
            dma((2, heads)),
            dma((2, heads)),
            dma((heads,)),
            dma((heads,)),
            dma((groups,)),
            dma((groups,)),
        ],
        compiler_params=pltpu.CompilerParams(
            collective_id=0, has_side_effects=True, vmem_limit_bytes=60 * 1024 * 1024
        ),
        name="layer",
    )(
        attn_query,
        attn_key,
        attn_value,
        delta_query,
        delta_key,
        delta_value,
        delta_gate,
        delta_beta,
        attn_gain,
        delta_gain,
    )


def solution(mesh):
    both = P("ctx", "head")
    return jax.shard_map(
        on_device,
        mesh=mesh,
        in_specs=(both,) * 8 + (P("head"),) * 2,
        out_specs=both,
        check_vma=False,
    )
```

profile of v0, /device:TPU:27, one launch (start us, length us, event | category | flops | bytes accessed | tf_op | source)
XLA Modules:
  0.0 139.6 jit_solution(13965600152715602928)
XLA Ops:
  0.0 1.6 %copy.11.gates_ref = f32[512,12]{1,0:T(8,128)} copy(f32[512,12]{0,1:T(8,128)} %param.16) | data formatting | bytes 49152 | tf_op args[6]
  1.6 1.6 %copy.12.betas_ref = f32[512,12]{1,0:T(8,128)} copy(f32[512,12]{0,1:T(8,128)} %param.17) | data formatting | bytes 49152 | tf_op args[7]
  3.2 133.7 %layer.1 = bf16[512,1536]{1,0:T(8,128)(2,1)} custom-call(bf16[512,1536]{1,0:T(8,128)(2,1)} %aq_ref.1, bf16[512,1536]{1,0:T(8,128)(2,1)} %ak_ref.1, bf16[512,1536]{1,0:T(8,128)(2,1)} %av_ref.1, bf16[512,1536]{1,0:T(8,128)(2,1)} %dq_ref.1, bf16[512,1536]{1,0:T(8,128)(2,1)} %dk_ref.1, bf16[512,1536]{1,0:T(8,128)(2,1)} %dv_ref.1, f32[512,12]{1,0:T(8,128)} %copy.11.gates_ref, ...), custom_call_target="tpu_custom_call" | custom-call | tf_op jit(solution)/shard_map/layer/pallas_call | solution.py:473
  137.0 2.7 %copy.14 = bf16[512,1536]{1,0:T(8,128)(2,1)} copy(bf16[512,1536]{1,0:T(8,128)(2,1)} %layer.1) | data formatting | bytes 3145728
where the time goes:
time: 140 us
  Pallas kernels  134 us (96%)
  local copies, waits for them, and re-layouts  5.86 us (4%)
    pallas_call x1, Pallas kernels, on_device(): pl.pallas_call(functools.partial(layer_kernel, contexts=lax.axis_size('ct...  134 us
    unnamed x3, local copies, waits for them, and re-layouts  5.86 us

commit v1 on v0

--- a/solution.py
+++ b/solution.py
@@ -12,8 +12,11 @@
 WINDOW = 1024
 CHUNK = 128
 QROWS = 256
-HALO_AHEAD = 1
-RELAY_LAG = 5
+FAR_AHEAD = 4
+NEAR_AHEAD = 2
+PASS_AHEAD = 1
+ATTEND_LAG = 1
+HOP = 1
 HEADS_STEP = 2
 
 epsilon = 1e-06
@@ -132,14 +135,16 @@
 
 
 def layer_kernel(
-    aq_ref, ak_ref, av_ref, dq_ref, dk_ref, dv_ref, gates_ref, betas_ref, again_ref, dgain_ref,
+    aq_hbm, ak_hbm, av_hbm, dq_hbm, dk_hbm, dv_hbm, gates_hbm, betas_hbm, again_ref, dgain_ref,
     mixed_hbm,
+    aq_ref, dq_ref, dk_ref, dv_ref, gates_ref, betas_ref,
     keys, vals, attn_out, delta_out, qeff, linear, offset, entering, leaving, attn_sq, delta_sq,
     sums_send, sums_recv, gate_ref, beta_ref, mixed_ref,
     out_sem, own_sem, far_send, far_recv, near_send, near_recv, relay_send, relay_recv, sums_ss, sums_rs,
+    query_sem, gates_sem, delta_sem,
     *, contexts, groups,
 ):
-    rows, width = aq_ref.shape
+    rows, width = aq_hbm.shape
     heads = width // DH
     me = lax.axis_index("ctx")
     group = lax.axis_index("head")
@@ -148,8 +153,10 @@
     back = WINDOW
     halves = rows // QROWS
     blocks = rows // CHUNK
-
-    both = ((0, ak_ref, keys), (1, av_ref, vals))
+    steps = heads // HEADS_STEP
+    units = 2 * heads
+
+    both = ((0, ak_hbm, keys), (1, av_hbm, vals))
     far_rows = pl.ds(0, rows)
     near_rows = pl.ds(rows, rows)
     own_rows = pl.ds(back, rows)
@@ -164,7 +171,7 @@
 
     def far_copy(h, kind, source, buffer):
         return pltpu.make_async_remote_copy(
-            src_ref=buffer.at[h, own_rows],
+            src_ref=source.at[:, lanes(h)],
             dst_ref=buffer.at[h, far_rows],
             send_sem=far_send.at[kind, h],
             recv_sem=far_recv.at[kind, h],
@@ -174,7 +181,7 @@
 
     def near_copy(h, kind, source, buffer):
         return pltpu.make_async_remote_copy(
-            src_ref=buffer.at[h, own_rows],
+            src_ref=source.at[:, lanes(h)],
             dst_ref=buffer.at[h, near_rows],
             send_sem=near_send.at[kind, h],
             recv_sem=near_recv.at[kind, h],
@@ -192,42 +199,63 @@
             device_id_type=pl.DeviceIdType.MESH,
         )
 
-    def relay_copy(h):
+    def pair(p):
+        return pl.ds(p * HEADS_STEP, HEADS_STEP)
+
+    def relay_copy(p):
         return pltpu.make_async_remote_copy(
-            src_ref=leaving.at[h],
-            dst_ref=entering.at[h],
-            send_sem=relay_send.at[h],
-            recv_sem=relay_recv.at[h],
+            src_ref=leaving.at[pair(p)],
+            dst_ref=entering.at[pair(p)],
+            send_sem=relay_send.at[p],
+            recv_sem=relay_recv.at[p],
             device_id={"ctx": lax.rem(me + 1, contexts)},
             device_id_type=pl.DeviceIdType.MESH,
         )
 
-    def send_halo(h):
-        @pl.when(h < heads)
-        def _():
-            @pl.when(me + 2 < contexts)
+    def pair_lanes(p):
+        return pl.ds(pl.multiple_of(p * HEADS_STEP * DH, HEADS_STEP * DH), HEADS_STEP * DH)
+
+    inputs = ((0, dq_hbm, dq_ref), (1, dk_hbm, dk_ref), (2, dv_hbm, dv_ref))
+
+    def delta_load(p, kind, source, buffer):
+        return pltpu.make_async_copy(
+            source.at[:, pair_lanes(p)], buffer.at[:, pair_lanes(p)], delta_sem.at[kind, p]
+        )
+
+    gate_load = pltpu.make_async_copy(gates_hbm, gates_ref, gates_sem.at[0])
+    beta_load = pltpu.make_async_copy(betas_hbm, betas_ref, gates_sem.at[1])
+    query_load = pltpu.make_async_copy(aq_hbm, aq_ref, query_sem.at[0])
+
+    def of_unit(u, action):
+        h = u // 2
+        for args in both:
+            @pl.when(lax.rem(u, 2) == args[0])
             def _():
-                for args in both:
-                    far_copy(h, *args).start()
-
-            @pl.when(even)
-            def _():
-                for args in both:
-                    near_copy(h, *args).start()
-
-    def forward(h):
-        @pl.when(odd & (me >= 3))
-        def _():
-            for args in both:
-                far_copy(h, *args).wait_recv()
-                forward_copy(h, *args).start()
-
-    def start_own(h, carry):
-        for args in both:
-            own_copy(h, *args).start()
-        return carry
-
-    lax.fori_loop(0, heads, start_own, 0)
+                action(h, *args)
+
+    def send_far(u):
+        @pl.when((u < units) & (me + 2 < contexts))
+        def _():
+            of_unit(u, lambda *args: far_copy(*args).start())
+
+    def send_near(u):
+        @pl.when((u < units) & even)
+        def _():
+            of_unit(u, lambda *args: near_copy(*args).start())
+
+    def send_on(u):
+        def action(*args):
+            far_copy(*args).wait_recv()
+            forward_copy(*args).start()
+
+        @pl.when((u < units) & odd & (me >= 3))
+        def _():
+            of_unit(u, action)
+
+    gate_load.start()
+    beta_load.start()
+    for args in inputs:
+        delta_load(0, *args).start()
 
     barrier = pltpu.get_barrier_semaphore()
     for by in (-2, -1, 1, 2):
@@ -241,16 +269,27 @@
             barrier, inc=1, device_id={"head": lax.rem(group + by, groups)},
             device_id_type=pl.DeviceIdType.MESH,
         )
+
+    def start_delta(p, carry):
+        for args in inputs:
+            delta_load(p, *args).start()
+        return carry
+
+    lax.fori_loop(1, steps, start_delta, 0)
+
     near_peers = jnp.minimum(me, 2) + jnp.minimum(contexts - 1 - me, 2)
     pl.semaphore_wait(barrier, near_peers + (groups - 1))
 
-    def wait_own(h, carry):
+    lax.fori_loop(0, FAR_AHEAD, lambda u, c: (send_far(u), c)[1], 0)
+    lax.fori_loop(0, NEAR_AHEAD, lambda u, c: (send_near(u), c)[1], 0)
+    query_load.start()
+
+    def start_own(h, carry):
         for args in both:
-            own_copy(h, *args).wait()
+            own_copy(h, *args).start()
         return carry
 
-    lax.fori_loop(0, heads, wait_own, 0)
-    lax.fori_loop(0, min(HALO_AHEAD, heads), lambda h, c: (send_halo(h), c)[1], 0)
+    lax.fori_loop(0, heads, start_own, 0)
 
     @pl.when(me < 2)
     def _():
@@ -265,32 +304,18 @@
         def clear(h, carry):
             keys[h, near_rows] = jnp.zeros((rows, DH), bf16)
             vals[h, near_rows] = jnp.zeros((rows, DH), bf16)
-            entering[h] = jnp.zeros((DH, DH), f32)
+            entering[h] = jnp.zeros((DH, DH), bf16)
             return carry
         lax.fori_loop(0, heads, clear, 0)
 
+    gate_load.wait()
+    beta_load.wait()
     gate_rows, beta_rows = gates_ref[...].T, betas_ref[...].T
     for h in range(heads):
         gate_ref[h] = gate_rows[h : h + 1]
         beta_ref[h] = beta_rows[h : h + 1]
     attn_sq[...] = jnp.zeros_like(attn_sq)
     delta_sq[...] = jnp.zeros_like(delta_sq)
-    steps = heads // HEADS_STEP
-
-    def delta_step(i, carry):
-        delta_heads(
-            i * HEADS_STEP, dq_ref, dk_ref, dv_ref, gate_ref, beta_ref,
-            delta_out, qeff, linear, offset,
-        )
-
-        @pl.when(i >= 1)
-        def _():
-            forward(i - 1)
-
-        send_halo(HALO_AHEAD + i)
-        return carry
-
-    lax.fori_loop(0, steps, delta_step, 0)
 
     scale = math.log2(math.e) / math.sqrt(DH)
     ri = lax.broadcasted_iota(jnp.int32, (QROWS, QROWS), 0)
@@ -324,57 +349,83 @@
         attn_out[h, q_rows] = out
         attn_sq[q_rows, :] += out * out
 
-    def relay(h):
+    def relay(p):
         @pl.when(me >= 1)
         def _():
-            relay_copy(h).wait_recv()
-
-        state = entering[h]
+            relay_copy(p).wait_recv()
 
         @pl.when(me + 1 < contexts)
         def _():
-            leaving[h] = dot3(linear[h], state) + offset[h]
-            relay_copy(h).start()
-
-        high, low = split(state)
-        q = qeff[h]
-        full = delta_out[h] + (dot(q, high) + dot(q, low))
-        delta_out[h] = full
-        delta_sq[...] += full * full
-
-    def step(j, carry):
-        h, b = j // halves, lax.rem(j, halves)
-
-        @pl.when(h < heads)
-        def _():
-            @pl.when(b == 0)
+            for e in range(HEADS_STEP):
+                h = p * HEADS_STEP + e
+                high, low = split(linear[h])
+                state = entering[h]
+                leaving[h] = (dot(high, state) + dot(low, state) + offset[h]).astype(bf16)
+            relay_copy(p).start()
+
+        for e in range(HEADS_STEP):
+            h = p * HEADS_STEP + e
+            full = delta_out[h] + dot(qeff[h], entering[h])
+            delta_out[h] = full
+            delta_sq[...] += full * full
+
+    def service(t):
+        q = t - HOP * me
+
+        @pl.when((q >= 0) & (lax.rem(q + 2 * contexts * HOP, 2) == 0) & (q < 2 * steps))
+        def _():
+            relay(q // 2)
+
+        send_far(t + FAR_AHEAD)
+        send_near(t + NEAR_AHEAD)
+
+        @pl.when(t == 0)
+        def _():
+            lax.fori_loop(0, PASS_AHEAD, lambda u, c: (send_on(u), c)[1], 0)
+
+        send_on(t + PASS_AHEAD)
+
+    def step(s, carry):
+        @pl.when(s < steps)
+        def _():
+            for args in inputs:
+                delta_load(s, *args).wait()
+            delta_heads(
+                s * HEADS_STEP, dq_ref, dk_ref, dv_ref, gate_ref, beta_ref,
+                delta_out, qeff, linear, offset,
+            )
+
+        service(2 * s)
+        h = s - ATTEND_LAG
+
+        @pl.when((h >= 0) & (h < heads))
+        def _():
+            @pl.when(h == 0)
             def _():
-                @pl.when(h >= steps - 1)
+                query_load.wait()
+
+            for args in both:
+                own_copy(h, *args).wait()
+
+                @pl.when((me >= 2) & jnp.logical_not(odd & (me >= 3)))
                 def _():
-                    forward(h)
-
-                for args in both:
-                    @pl.when((me >= 2) & jnp.logical_not(odd & (me >= 3)))
-                    def _():
-                        far_copy(h, *args).wait_recv()
-
-                    @pl.when(me >= 1)
-                    def _():
-                        near_copy(h, *args).wait_recv()
-
-                send_halo(h + HALO_AHEAD + steps)
-
-            attend(h, b)
-
-        r = j - RELAY_LAG * me
-
-        @pl.when((r >= 0) & (r < heads))
-        def _():
-            relay(r)
+                    far_copy(h, *args).wait_recv()
+
+                @pl.when(me >= 1)
+                def _():
+                    near_copy(h, *args).wait_recv()
+
+            attend(h, 0)
+
+        service(2 * s + 1)
+
+        @pl.when((h >= 0) & (h < heads))
+        def _():
+            lax.fori_loop(1, halves, lambda b, c: (attend(h, b), c)[1], 0)
 
         return carry
 
-    turns = max(heads * halves, RELAY_LAG * (contexts - 1) + heads)
+    turns = max(heads + ATTEND_LAG, steps + (HOP * (contexts - 1)) // 2 + 1)
     lax.fori_loop(0, turns, step, 0)
 
     dr = lax.broadcasted_iota(jnp.int32, (CHUNK, CHUNK), 0)
@@ -442,13 +493,13 @@
             def _():
                 forward_copy(h, *args).wait_send()
 
-        @pl.when(me + 1 < contexts)
-        def _():
-            relay_copy(h).wait_send()
-
         return carry
 
     lax.fori_loop(0, heads, drain, 0)
+
+    @pl.when(me + 1 < contexts)
+    def _():
+        lax.fori_loop(0, steps, lambda p, c: (relay_copy(p).wait_send(), c)[1], 0)
 
 
 def on_device(
@@ -472,10 +523,16 @@
     dma = pltpu.SemaphoreType.DMA
     return pl.pallas_call(
         functools.partial(layer_kernel, contexts=lax.axis_size("ctx"), groups=groups),
-        in_specs=[vmem, hbm, hbm] + [vmem] * 7,
+        in_specs=[hbm] * 8 + [vmem] * 2,
         out_specs=hbm,
         out_shape=jax.ShapeDtypeStruct((rows, width), bf16),
         scratch_shapes=[
+            pltpu.VMEM((rows, width), bf16),
+            pltpu.VMEM((rows, width), bf16),
+            pltpu.VMEM((rows, width), bf16),
+            pltpu.VMEM((rows, width), bf16),
+            pltpu.VMEM((rows, heads), f32),
+            pltpu.VMEM((rows, heads), f32),
             pltpu.VMEM((heads, WINDOW + rows, DH), bf16),
             pltpu.VMEM((heads, WINDOW + rows, DH), bf16),
             pltpu.VMEM((heads, rows, DH), f32),
@@ -483,8 +540,8 @@
             pltpu.VMEM((heads, rows, DH), bf16),
             pltpu.VMEM((heads, DH, DH), f32),
             pltpu.VMEM((heads, DH, DH), f32),
-            pltpu.VMEM((heads, DH, DH), f32),
-            pltpu.VMEM((heads, DH, DH), f32),
+            pltpu.VMEM((heads, DH, DH), bf16),
+            pltpu.VMEM((heads, DH, DH), bf16),
             pltpu.VMEM((rows, DH), f32),
             pltpu.VMEM((rows, DH), f32),
             pltpu.VMEM((lines, CHUNK), f32),
@@ -498,10 +555,13 @@
             dma((2, heads)),
             dma((2, heads)),
             dma((2, heads)),
-            dma((heads,)),
-            dma((heads,)),
+            dma((heads // HEADS_STEP,)),
+            dma((heads // HEADS_STEP,)),
             dma((groups,)),
             dma((groups,)),
+            dma((1,)),
+            dma((2,)),
+            dma((3, heads // HEADS_STEP)),
         ],
         compiler_params=pltpu.CompilerParams(
             collective_id=0, has_side_effects=True, vmem_limit_bytes=60 * 1024 * 1024

time: 140 us -> 108 us (0.77)
  Pallas kernels: 134 us -> 101 us
    pallas_call x1, Pallas kernels: 134 us -> 101 us  [on_device(): pl.pallas_call(functools.partial(layer_kernel, contexts=lax.axis_size('ct...]
where the time goes in v1:
time: 108 us; the launch traced here: 107 us
  Pallas kernels  101 us (94%)
  local copies, waits for them, and re-layouts  5.86 us (5%)
    pallas_call x1, Pallas kernels, on_device(): pl.pallas_call(functools.partial(layer_kernel, contexts=lax.axis_size('ct...  101 us
    unnamed x3, local copies, waits for them, and re-layouts  5.86 us

profile of v1, /device:TPU:27, one launch (start us, length us, event | category | flops | bytes accessed | tf_op | source)
XLA Modules:
  0.0 106.6 jit_solution(5537231186143971799)
XLA Ops:
  0.0 1.6 %copy.11.gates_hbm = f32[512,12]{1,0:T(8,128)} copy(f32[512,12]{0,1:T(8,128)} %param.16) | data formatting | bytes 49152 | tf_op args[6]
  1.6 1.6 %copy.12.betas_hbm = f32[512,12]{1,0:T(8,128)} copy(f32[512,12]{0,1:T(8,128)} %param.17) | data formatting | bytes 49152 | tf_op args[7]
  3.2 100.7 %layer.1 = bf16[512,1536]{1,0:T(8,128)(2,1)} custom-call(bf16[512,1536]{1,0:T(8,128)(2,1)} %aq_hbm.1, bf16[512,1536]{1,0:T(8,128)(2,1)} %ak_hbm.1, bf16[512,1536]{1,0:T(8,128)(2,1)} %av_hbm.1, bf16[512,1536]{1,0:T(8,128)(2,1)} %dq_hbm.1, bf16[512,1536]{1,0:T(8,128)(2,1)} %dk_hbm.1, bf16[512,1536]{1,0:T(8,128)(2,1)} %dv_hbm.1, f32[512,12]{1,0:T(8,128)} %copy.11.gates_hbm, ...), custom_call_target="tpu_custom_call" | custom-call | tf_op jit(solution)/shard_map/layer/pallas_call | solution.py:524
  103.9 2.7 %copy.14 = bf16[512,1536]{1,0:T(8,128)(2,1)} copy(bf16[512,1536]{1,0:T(8,128)(2,1)} %layer.1) | data formatting | bytes 3145728

commit v2 on v1

--- a/solution.py
+++ b/solution.py
@@ -12,11 +12,12 @@
 WINDOW = 1024
 CHUNK = 128
 QROWS = 256
-FAR_AHEAD = 4
+FAR_AHEAD = 3
 NEAR_AHEAD = 2
 PASS_AHEAD = 1
 ATTEND_LAG = 1
 HOP = 1
+RATE = 5
 HEADS_STEP = 2
 
 epsilon = 1e-06
@@ -49,7 +50,7 @@
     return lax.rsqrt(mean + epsilon) / math.sqrt(DH)
 
 
-def delta_heads(first, q_ref, k_ref, v_ref, gate_ref, beta_ref, out_ref, qeff_ref, lin_ref, off_ref):
+def delta_heads(first, between, q_ref, k_ref, v_ref, gate_ref, beta_ref, out_ref, qeff_ref, lin_ref, off_ref):
     rows = q_ref.shape[0]
     chunks = rows // CHUNK
     ri = lax.broadcasted_iota(jnp.int32, (CHUNK, CHUNK), 0)
@@ -104,6 +105,7 @@
             t = terms[u]
             t["inv"] = t["inv"] - dot1(t["inv"], t["tmp"])
         size *= 2
+    between()
     states = [None] * HEADS_STEP
     for c in range(chunks):
         rs = slice(c * CHUNK, (c + 1) * CHUNK)
@@ -135,12 +137,12 @@
 
 
 def layer_kernel(
-    aq_hbm, ak_hbm, av_hbm, dq_hbm, dk_hbm, dv_hbm, gates_hbm, betas_hbm, again_ref, dgain_ref,
-    mixed_hbm,
+    aq_hbm, ak_hbm, av_hbm, dq_hbm, dk_hbm, dv_hbm, gates_hbm, betas_hbm, again_hbm, dgain_hbm,
+    mixed_ref,
     aq_ref, dq_ref, dk_ref, dv_ref, gates_ref, betas_ref,
     keys, vals, attn_out, delta_out, qeff, linear, offset, entering, leaving, attn_sq, delta_sq,
-    sums_send, sums_recv, gate_ref, beta_ref, mixed_ref,
-    out_sem, own_sem, far_send, far_recv, near_send, near_recv, relay_send, relay_recv, sums_ss, sums_rs,
+    sums_send, sums_recv, gate_ref, beta_ref, again_ref, dgain_ref,
+    gain_sem, own_sem, far_send, far_recv, near_send, near_recv, relay_send, relay_recv, sums_ss, sums_rs,
     query_sem, gates_sem, delta_sem,
     *, contexts, groups,
 ):
@@ -252,6 +254,25 @@
         def _():
             of_unit(u, action)
 
+    def issued(k, ahead):
+        early = 3 * steps
+        count = (jnp.minimum(k, early) * RATE) // 6 + jnp.maximum(k - early, 0) + ahead
+        return jnp.minimum(count, units)
+
+    def advance(k, send, ahead):
+        done = jnp.where(k == 0, 0, issued(jnp.maximum(k - 1, 0), ahead))
+        lax.fori_loop(done, issued(k, ahead), lambda u, c: (send(u), c)[1], 0)
+
+    def issue(k):
+        advance(k, send_far, FAR_AHEAD)
+        advance(k, send_near, NEAR_AHEAD)
+
+        @pl.when(k == 1)
+        def _():
+            advance(0, send_on, PASS_AHEAD)
+
+        advance(k, send_on, PASS_AHEAD)
+
     gate_load.start()
     beta_load.start()
     for args in inputs:
@@ -280,9 +301,15 @@
     near_peers = jnp.minimum(me, 2) + jnp.minimum(contexts - 1 - me, 2)
     pl.semaphore_wait(barrier, near_peers + (groups - 1))
 
-    lax.fori_loop(0, FAR_AHEAD, lambda u, c: (send_far(u), c)[1], 0)
-    lax.fori_loop(0, NEAR_AHEAD, lambda u, c: (send_near(u), c)[1], 0)
+    advance(0, send_far, FAR_AHEAD)
+    advance(0, send_near, NEAR_AHEAD)
     query_load.start()
+    gain_loads = (
+        pltpu.make_async_copy(again_hbm, again_ref, gain_sem.at[0]),
+        pltpu.make_async_copy(dgain_hbm, dgain_ref, gain_sem.at[1]),
+    )
+    for load in gain_loads:
+        load.start()
 
     def start_own(h, carry):
         for args in both:
@@ -310,10 +337,9 @@
 
     gate_load.wait()
     beta_load.wait()
-    gate_rows, beta_rows = gates_ref[...].T, betas_ref[...].T
     for h in range(heads):
-        gate_ref[h] = gate_rows[h : h + 1]
-        beta_ref[h] = beta_rows[h : h + 1]
+        gate_ref[h] = gates_ref[h : h + 1]
+        beta_ref[h] = betas_ref[h : h + 1]
     attn_sq[...] = jnp.zeros_like(attn_sq)
     delta_sq[...] = jnp.zeros_like(delta_sq)
 
@@ -376,22 +402,22 @@
         def _():
             relay(q // 2)
 
-        send_far(t + FAR_AHEAD)
-        send_near(t + NEAR_AHEAD)
-
-        @pl.when(t == 0)
-        def _():
-            lax.fori_loop(0, PASS_AHEAD, lambda u, c: (send_on(u), c)[1], 0)
-
-        send_on(t + PASS_AHEAD)
-
     def step(s, carry):
-        @pl.when(s < steps)
+        early = s < steps
+        mark = jnp.where(early, 3 * s, 3 * steps + 2 * (s - steps))
+
+        @pl.when(jnp.logical_not(early))
+        def _():
+            issue(mark + 1)
+
+        @pl.when(early)
         def _():
             for args in inputs:
                 delta_load(s, *args).wait()
+
+            issue(mark + 1)
             delta_heads(
-                s * HEADS_STEP, dq_ref, dk_ref, dv_ref, gate_ref, beta_ref,
+                s * HEADS_STEP, lambda: issue(mark + 2), dq_ref, dk_ref, dv_ref, gate_ref, beta_ref,
                 delta_out, qeff, linear, offset,
             )
 
@@ -418,6 +444,7 @@
             attend(h, 0)
 
         service(2 * s + 1)
+        issue(mark + jnp.where(early, 3, 2))
 
         @pl.when((h >= 0) & (h < heads))
         def _():
@@ -425,8 +452,10 @@
 
         return carry
 
-    turns = max(heads + ATTEND_LAG, steps + (HOP * (contexts - 1)) // 2 + 1)
+    turns = max(heads + ATTEND_LAG, steps + (HOP * (contexts - 1)) // 2, steps + heads)
     lax.fori_loop(0, turns, step, 0)
+    for load in gain_loads:
+        load.wait()
 
     dr = lax.broadcasted_iota(jnp.int32, (CHUNK, CHUNK), 0)
     dc = lax.broadcasted_iota(jnp.int32, (CHUNK, CHUNK), 1)
@@ -457,10 +486,6 @@
         whole = whole + sums_recv[by]
     scales = lax.rsqrt(whole / (width * groups) + epsilon) * 0.5
 
-    def out_copy(b):
-        span = pl.ds(b * CHUNK, CHUNK)
-        return pltpu.make_async_copy(mixed_ref.at[span], mixed_hbm.at[span], out_sem.at[b])
-
     for b in range(blocks):
         rs = slice(b * CHUNK, (b + 1) * CHUNK)
         sa = jnp.sum(jnp.where(eye, scales[b : b + 1], 0.0), axis=1, keepdims=True)
@@ -472,10 +497,7 @@
             mixed_ref[rs, cs] = (
                 again_ref[cs][None, :] * attn_out[h, rs] * sa + dgain_ref[cs][None, :] * delta_out[h, rs] * sd
             ).astype(bf16)
-        out_copy(b).start()
-
-    for b in range(blocks):
-        out_copy(b).wait()
+
     for by in range(1, groups):
         sums_copy(by).wait_send()
 
@@ -518,21 +540,20 @@
     heads = width // DH
     groups = lax.axis_size("head")
     lines = 2 * rows // CHUNK
-    vmem = pl.BlockSpec(memory_space=pltpu.VMEM)
-    hbm = pl.BlockSpec(memory_space=pl.ANY)
+    hbm = pl.BlockSpec(memory_space=pltpu.HBM)
     dma = pltpu.SemaphoreType.DMA
     return pl.pallas_call(
         functools.partial(layer_kernel, contexts=lax.axis_size("ctx"), groups=groups),
-        in_specs=[hbm] * 8 + [vmem] * 2,
-        out_specs=hbm,
-        out_shape=jax.ShapeDtypeStruct((rows, width), bf16),
+        in_specs=[hbm] * 10,
+        out_specs=pl.BlockSpec(memory_space=pltpu.VMEM),
+        out_shape=pltpu.VMEM((rows, width), bf16),
         scratch_shapes=[
             pltpu.VMEM((rows, width), bf16),
             pltpu.VMEM((rows, width), bf16),
             pltpu.VMEM((rows, width), bf16),
             pltpu.VMEM((rows, width), bf16),
-            pltpu.VMEM((rows, heads), f32),
-            pltpu.VMEM((rows, heads), f32),
+            pltpu.VMEM((heads, rows), f32),
+            pltpu.VMEM((heads, rows), f32),
             pltpu.VMEM((heads, WINDOW + rows, DH), bf16),
             pltpu.VMEM((heads, WINDOW + rows, DH), bf16),
             pltpu.VMEM((heads, rows, DH), f32),
@@ -548,8 +569,9 @@
             pltpu.VMEM((groups, lines, CHUNK), f32),
             pltpu.VMEM((heads, 1, rows), f32),
             pltpu.VMEM((heads, 1, rows), f32),
-            pltpu.VMEM((rows, width), bf16),
-            dma((rows // CHUNK,)),
+            pltpu.VMEM((width,), f32),
+            pltpu.VMEM((width,), f32),
+            dma((2,)),
             dma((2, heads)),
             dma((2, heads)),
             dma((2, heads)),
@@ -564,7 +586,7 @@
             dma((3, heads // HEADS_STEP)),
         ],
         compiler_params=pltpu.CompilerParams(
-            collective_id=0, has_side_effects=True, vmem_limit_bytes=60 * 1024 * 1024
+            collective_id=0, has_side_effects=True, vmem_limit_bytes=67043328 - 2 * rows * width - 16384
         ),
         name="layer",
     )(
@@ -574,8 +596,8 @@
         delta_query,
         delta_key,
         delta_value,
-        delta_gate,
-        delta_beta,
+        delta_gate.T,
+        delta_beta.T,
         attn_gain,
         delta_gain,
     )

time: 108 us -> 99.1 us (0.918); the launches traced: 107 us -> 99 us
  local copies, waits for them, and re-layouts: 5.86 us -> 1.15 us
  Pallas kernels: 101 us -> 97.9 us
    unnamed x3 -> x1, local copies, waits for them, and re-layouts: 5.86 us -> 1.15 us
    pallas_call x1, Pallas kernels: 101 us -> 97.9 us  [on_device(): pl.pallas_call(functools.partial(layer_kernel, contexts=lax.axis_size('ct...]
where the time goes in v2:
time: 99.1 us; the launch traced here: 99 us
  Pallas kernels  97.9 us (99%)
  local copies, waits for them, and re-layouts  1.15 us (1%)
    pallas_call x1, Pallas kernels, on_device(): pl.pallas_call(functools.partial(layer_kernel, contexts=lax.axis_size('ct...  97.9 us

profile of v2, /device:TPU:27, one launch (start us, length us, event | category | flops | bytes accessed | tf_op | source)
XLA Modules:
  0.0 99.0 jit_solution(4903864085988202142)
XLA Ops:
  0.0 97.9 %layer.1 = bf16[512,1536]{1,0:T(8,128)(2,1)S(1)} custom-call(bf16[512,1536]{1,0:T(8,128)(2,1)} %aq_hbm.1, bf16[512,1536]{1,0:T(8,128)(2,1)} %ak_hbm.1, bf16[512,1536]{1,0:T(8,128)(2,1)} %av_hbm.1, bf16[512,1536]{1,0:T(8,128)(2,1)} %dq_hbm.1, bf16[512,1536]{1,0:T(8,128)(2,1)} %dk_hbm.1, bf16[512,1536]{1,0:T(8,128)(2,1)} %dv_hbm.1, f32[12,512]{1,0:T(8,128)} %bitcast.2, ...), custom_call_target="tpu_custom_call" | custom-call | tf_op jit(solution)/shard_map/layer/pallas_call | solution.py:545
  97.9 1.1 %copy.12 = bf16[512,1536]{1,0:T(8,128)(2,1)} copy(bf16[512,1536]{1,0:T(8,128)(2,1)S(1)} %layer.1) | data formatting | bytes 3145728

commit v3 on v2

--- a/solution.py
+++ b/solution.py
@@ -13,11 +13,12 @@
 CHUNK = 128
 QROWS = 256
 FAR_AHEAD = 3
-NEAR_AHEAD = 2
+NEAR_AHEAD = 1
 PASS_AHEAD = 1
 ATTEND_LAG = 1
-HOP = 1
+LATE_STRIDE = 3
 RATE = 5
+STAGE_AT = 6
 HEADS_STEP = 2
 
 epsilon = 1e-06
@@ -143,7 +144,7 @@
     keys, vals, attn_out, delta_out, qeff, linear, offset, entering, leaving, attn_sq, delta_sq,
     sums_send, sums_recv, gate_ref, beta_ref, again_ref, dgain_ref,
     gain_sem, own_sem, far_send, far_recv, near_send, near_recv, relay_send, relay_recv, sums_ss, sums_rs,
-    query_sem, gates_sem, delta_sem,
+    query_sem, gates_sem, delta_sem, stage, stage_send, stage_recv, hop_send,
     *, contexts, groups,
 ):
     rows, width = aq_hbm.shape
@@ -201,6 +202,29 @@
             device_id_type=pl.DeviceIdType.MESH,
         )
 
+    def stage_copy(kind, source, buffer):
+        return pltpu.make_async_remote_copy(
+            src_ref=source.at[:, lanes(heads - 1)],
+            dst_ref=stage.at[kind],
+            send_sem=stage_send.at[kind],
+            recv_sem=stage_recv.at[kind],
+            device_id={"ctx": lax.rem(me + contexts - 1, contexts)},
+            device_id_type=pl.DeviceIdType.MESH,
+        )
+
+    def hop_copy(kind, source, buffer):
+        return pltpu.make_async_remote_copy(
+            src_ref=stage.at[kind],
+            dst_ref=buffer.at[heads - 1, near_rows],
+            send_sem=hop_send.at[kind],
+            recv_sem=near_recv.at[kind, heads - 1],
+            device_id={"ctx": lax.rem(me + 2, contexts)},
+            device_id_type=pl.DeviceIdType.MESH,
+        )
+
+    stages = odd & (me + 1 < contexts)
+    hops = even & (me + 2 < contexts)
+
     def pair(p):
         return pl.ds(p * HEADS_STEP, HEADS_STEP)
 
@@ -250,7 +274,7 @@
             far_copy(*args).wait_recv()
             forward_copy(*args).start()
 
-        @pl.when((u < units) & odd & (me >= 3))
+        @pl.when((u < units - 2) & odd & (me >= 3))
         def _():
             of_unit(u, action)
 
@@ -263,15 +287,33 @@
         done = jnp.where(k == 0, 0, issued(jnp.maximum(k - 1, 0), ahead))
         lax.fori_loop(done, issued(k, ahead), lambda u, c: (send(u), c)[1], 0)
 
+    def issue_free(k):
+        @pl.when(even)
+        def _():
+            advance(k, send_far, FAR_AHEAD)
+
+        @pl.when(k == 1)
+        def _():
+            advance(0, send_on, PASS_AHEAD)
+
+        advance(k, send_on, PASS_AHEAD)
+
+        @pl.when((k == STAGE_AT) & hops)
+        def _():
+            for args in both:
+                stage_copy(*args).wait_recv()
+                hop_copy(*args).start()
+
+    def issue_tight(k):
+        @pl.when(odd)
+        def _():
+            advance(k, send_far, FAR_AHEAD)
+
+        advance(k, send_near, NEAR_AHEAD)
+
     def issue(k):
-        advance(k, send_far, FAR_AHEAD)
-        advance(k, send_near, NEAR_AHEAD)
-
-        @pl.when(k == 1)
-        def _():
-            advance(0, send_on, PASS_AHEAD)
-
-        advance(k, send_on, PASS_AHEAD)
+        issue_tight(k)
+        issue_free(k)
 
     gate_load.start()
     beta_load.start()
@@ -300,6 +342,11 @@
 
     near_peers = jnp.minimum(me, 2) + jnp.minimum(contexts - 1 - me, 2)
     pl.semaphore_wait(barrier, near_peers + (groups - 1))
+
+    @pl.when(stages)
+    def _():
+        for args in both:
+            stage_copy(*args).start()
 
     advance(0, send_far, FAR_AHEAD)
     advance(0, send_near, NEAR_AHEAD)
@@ -396,9 +443,15 @@
             delta_sq[...] += full * full
 
     def service(t):
-        q = t - HOP * me
-
-        @pl.when((q >= 0) & (lax.rem(q + 2 * contexts * HOP, 2) == 0) & (q < 2 * steps))
+        over = t - 2 * steps
+        late = over >= 0
+        turn = jnp.where(late, 2 * steps + over // LATE_STRIDE, t)
+        q = turn - me
+
+        @pl.when(
+            (q >= 0) & (lax.rem(q + 2 * contexts, 2) == 0) & (q < 2 * steps)
+            & (jnp.logical_not(late) | (lax.rem(over + 2 * steps * LATE_STRIDE, LATE_STRIDE) == 0))
+        )
         def _():
             relay(q // 2)
 
@@ -433,7 +486,7 @@
             for args in both:
                 own_copy(h, *args).wait()
 
-                @pl.when((me >= 2) & jnp.logical_not(odd & (me >= 3)))
+                @pl.when((me >= 2) & jnp.logical_not(odd & (me >= 3) & (h < heads - 1)))
                 def _():
                     far_copy(h, *args).wait_recv()
 
@@ -443,8 +496,10 @@
 
             attend(h, 0)
 
+        third = mark + jnp.where(early, 3, 2)
+        issue_free(third)
         service(2 * s + 1)
-        issue(mark + jnp.where(early, 3, 2))
+        issue_tight(third)
 
         @pl.when((h >= 0) & (h < heads))
         def _():
@@ -452,7 +507,8 @@
 
         return carry
 
-    turns = max(heads + ATTEND_LAG, steps + (HOP * (contexts - 1)) // 2, steps + heads)
+    last_turn = max(2 * (steps - 1) + contexts - 1 - 2 * steps, 0)
+    turns = max(heads + ATTEND_LAG, steps + heads, steps + (last_turn * LATE_STRIDE) // 2 + 1)
     lax.fori_loop(0, turns, step, 0)
     for load in gain_loads:
         load.wait()
@@ -511,9 +567,17 @@
             def _():
                 near_copy(h, *args).wait_send()
 
-            @pl.when(odd & (me >= 3))
+            @pl.when(odd & (me >= 3) & (h < heads - 1))
             def _():
                 forward_copy(h, *args).wait_send()
+
+            @pl.when((h == 0) & stages)
+            def _():
+                stage_copy(*args).wait_send()
+
+            @pl.when((h == 0) & hops)
+            def _():
+                hop_copy(*args).wait_send()
 
         return carry
 
@@ -584,6 +648,10 @@
             dma((1,)),
             dma((2,)),
             dma((3, heads // HEADS_STEP)),
+            pltpu.VMEM((2, rows, DH), bf16),
+            dma((2,)),
+            dma((2,)),
+            dma((2,)),
         ],
         compiler_params=pltpu.CompilerParams(
             collective_id=0, has_side_effects=True, vmem_limit_bytes=67043328 - 2 * rows * width - 16384

time: 99.1 us -> 97.8 us (0.987)
  Pallas kernels: 97.9 us -> 96.5 us
    pallas_call x1, Pallas kernels: 97.9 us -> 96.5 us  [on_device(): pl.pallas_call(functools.partial(layer_kernel, contexts=lax.axis_size('ct...]
where the time goes in v3:
time: 97.8 us; the launch traced here: 97.6 us
  Pallas kernels  96.5 us (99%)
  local copies, waits for them, and re-layouts  1.15 us (1%)
    pallas_call x1, Pallas kernels, on_device(): pl.pallas_call(functools.partial(layer_kernel, contexts=lax.axis_size('ct...  96.5 us

profile of v3, /device:TPU:27, one launch (start us, length us, event | category | flops | bytes accessed | tf_op | source)
XLA Modules:
  0.0 97.6 jit_solution(3321458707736790211)
XLA Ops:
  0.0 96.5 %layer.1 = bf16[512,1536]{1,0:T(8,128)(2,1)S(1)} custom-call(bf16[512,1536]{1,0:T(8,128)(2,1)} %aq_hbm.1, bf16[512,1536]{1,0:T(8,128)(2,1)} %ak_hbm.1, bf16[512,1536]{1,0:T(8,128)(2,1)} %av_hbm.1, bf16[512,1536]{1,0:T(8,128)(2,1)} %dq_hbm.1, bf16[512,1536]{1,0:T(8,128)(2,1)} %dk_hbm.1, bf16[512,1536]{1,0:T(8,128)(2,1)} %dv_hbm.1, f32[12,512]{1,0:T(8,128)} %bitcast.2, ...), custom_call_target="tpu_custom_call" | custom-call | tf_op jit(solution)/shard_map/layer/pallas_call | solution.py:609
  96.5 1.1 %copy.12 = bf16[512,1536]{1,0:T(8,128)(2,1)} copy(bf16[512,1536]{1,0:T(8,128)(2,1)S(1)} %layer.1) | data formatting | bytes 3145728

commit v4 on v3

--- a/solution.py
+++ b/solution.py
@@ -459,10 +459,6 @@
         early = s < steps
         mark = jnp.where(early, 3 * s, 3 * steps + 2 * (s - steps))
 
-        @pl.when(jnp.logical_not(early))
-        def _():
-            issue(mark + 1)
-
         @pl.when(early)
         def _():
             for args in inputs:
@@ -474,7 +470,16 @@
                 delta_out, qeff, linear, offset,
             )
 
+        @pl.when(jnp.logical_not(early))
+        def _():
+            issue_free(mark + 1)
+
         service(2 * s)
+
+        @pl.when(jnp.logical_not(early))
+        def _():
+            issue_tight(mark + 1)
+
         h = s - ATTEND_LAG
 
         @pl.when((h >= 0) & (h < heads))
@@ -536,6 +541,10 @@
 
     for by in range(1, groups):
         sums_copy(by).start()
+    for h in range(heads):
+        cs = slice(h * DH, (h + 1) * DH)
+        attn_out[h] = again_ref[cs][None, :] * attn_out[h]
+        delta_out[h] = dgain_ref[cs][None, :] * delta_out[h]
     whole = mine
     for by in range(1, groups):
         sums_copy(by).wait_recv()
@@ -551,7 +560,7 @@
         for h in range(heads):
             cs = slice(h * DH, (h + 1) * DH)
             mixed_ref[rs, cs] = (
-                again_ref[cs][None, :] * attn_out[h, rs] * sa + dgain_ref[cs][None, :] * delta_out[h, rs] * sd
+                attn_out[h, rs] * sa + delta_out[h, rs] * sd
             ).astype(bf16)
 
     for by in range(1, groups):

time: 97.8 us -> 97.6 us (level)
  no operation moved by 1% of the time
where the time goes in v4:
time: 97.6 us; the launch traced here: 97.5 us
  Pallas kernels  96.3 us (99%)
  local copies, waits for them, and re-layouts  1.15 us (1%)
    pallas_call x1, Pallas kernels, on_device(): pl.pallas_call(functools.partial(layer_kernel, contexts=lax.axis_size('ct...  96.3 us

profile of v4, /device:TPU:27, one launch (start us, length us, event | category | flops | bytes accessed | tf_op | source)
XLA Modules:
  0.0 97.5 jit_solution(10607369828188044375)
XLA Ops:
  0.0 96.3 %layer.1 = bf16[512,1536]{1,0:T(8,128)(2,1)S(1)} custom-call(bf16[512,1536]{1,0:T(8,128)(2,1)} %aq_hbm.1, bf16[512,1536]{1,0:T(8,128)(2,1)} %ak_hbm.1, bf16[512,1536]{1,0:T(8,128)(2,1)} %av_hbm.1, bf16[512,1536]{1,0:T(8,128)(2,1)} %dq_hbm.1, bf16[512,1536]{1,0:T(8,128)(2,1)} %dk_hbm.1, bf16[512,1536]{1,0:T(8,128)(2,1)} %dv_hbm.1, f32[12,512]{1,0:T(8,128)} %bitcast.2, ...), custom_call_target="tpu_custom_call" | custom-call | tf_op jit(solution)/shard_map/layer/pallas_call | solution.py:618
  96.3 1.1 %copy.12 = bf16[512,1536]{1,0:T(8,128)(2,1)} copy(bf16[512,1536]{1,0:T(8,128)(2,1)S(1)} %layer.1) | data formatting | bytes 3145728
